TPU v7x, 32 devices: a whole 2x2x4 slice. The times are simulated.
32 devices in a mesh: rep: 4 (over y, core), seq: 2 (over x), ctx: 4 (over z).
Axes of the slice: x: 2, y: 2, z: 4, core: 2. Of those that a mesh axis runs over, the one named last changes fastest.
Arguments:
- tokens: bfloat16 [8192, 2048], P(('rep', 'seq', 'ctx')), may hold values from -6 to 6
- cotangent: bfloat16 [8192, 2048], P(('rep', 'seq', 'ctx')), may hold values from -6 to 6
- document_index: int32 [8192], P(('rep', 'seq')), may hold values from 0 to 10, as said below
- padding_token_mask: int32 [8192], P(('rep', 'seq')), may hold values from 0 to 1, as said below
- attention_gain: bfloat16 [2048], P(('seq', 'ctx')), may hold values from 0.099609375 to 1.8984375
- projection_weight: bfloat16 [2048, 6144], P(('seq', 'ctx')), may hold values from -0.125 to 0.125
- head_gain: bfloat16 [2, 128], replicated, may hold values from 0.099609375 to 1.8984375
- out_weight: bfloat16 [2048, 2048], P(('seq', 'ctx')), may hold values from -2 to 2
- feedforward_gain: bfloat16 [2048], P(('seq', 'ctx')), may hold values from 0.099609375 to 1.8984375
- gate_weight: bfloat16 [2048, 6144], P(('seq', 'ctx')), may hold values from -0.125 to 0.125
- up_weight: bfloat16 [2048, 6144], P(('seq', 'ctx')), may hold values from -0.125 to 0.125
- down_weight: bfloat16 [2048, 6144], P(('seq', 'ctx')), may hold values from -0.078125 to 0.078125
Outputs:
- layer_out: bfloat16 [8192, 2048], P(('rep', 'seq', 'ctx'))
- tokens_grad: bfloat16 [8192, 2048], P(('rep', 'seq', 'ctx'))
- attention_gain_grad: float32 [2048], P(('seq', 'ctx'))
- proj_weight_grad: float32 [2048, 6144], P(('seq', 'ctx'))
- head_gain_grad: float32 [2, 128], replicated
- out_weight_grad: float32 [2048, 2048], P(('seq', 'ctx'))
- feedforward_gain_grad: float32 [2048], P(('seq', 'ctx'))
- gate_weight_grad: float32 [2048, 6144], P(('seq', 'ctx'))
- up_weight_grad: float32 [2048, 6144], P(('seq', 'ctx'))
- down_weight_grad: float32 [2048, 6144], P(('seq', 'ctx'))
Inputs may be any that keep to these rules, and one draw needn't show every extreme that they name: `document_index`: along each sequence of 1024 tokens the ids never fall. `padding_token_mask`: the zeros of a sequence form one run at its end.
All inputs are finite; a program needn't handle non-finite values.
Results may differ from a plain program's by a relative error of at most 0.02.
Values may be sent and summed in bfloat16 or wider, within the bound.
A program may use at most 640 MiB of HBM per device.

v0:
```python
import jax
import jax.numpy as jnp
from jax import lax
from jax.sharding import PartitionSpec as P

QUERY_HEADS = 16
KEY_VALUE_HEADS = 8
HEAD_SIZE = 128
norm_epsilon = 1e-06
rope_base = 1000000.0
masked_value = -1e30
contract_rows = (((0,), (0,)), ((), ()))
contract_cols = (((1,), (1,)), ((), ()))


def rope_tables(positions):
    half_size = HEAD_SIZE // 2
    frequency = rope_base ** (-2.0 * jnp.arange(half_size, dtype=jnp.float32) / HEAD_SIZE)
    angles = positions.astype(jnp.float32)[:, None, None] * frequency[None, None, :]
    return (jnp.cos(angles), jnp.sin(angles))


def rotate(value_rows, cosine_table, sine_table):
    half_size = value_rows.shape[-1] // 2
    first_half = value_rows[..., :half_size]
    second_half = value_rows[..., half_size:]
    return jnp.concatenate(
        [
            first_half * cosine_table - second_half * sine_table,
            second_half * cosine_table + first_half * sine_table,
        ],
        axis=-1,
    )


def inverse_rotation(grads, cosine_table, sine_table):
    half_size = grads.shape[-1] // 2
    first_half = grads[..., :half_size]
    second_half = grads[..., half_size:]
    return jnp.concatenate(
        [
            first_half * cosine_table + second_half * sine_table,
            second_half * cosine_table - first_half * sine_table,
        ],
        axis=-1,
    )


def head_norm(value_rows, gain):
    root_factor = lax.rsqrt(
        jnp.mean(value_rows * value_rows, axis=-1, keepdims=True) + norm_epsilon
    )
    unit_values = value_rows * root_factor
    return (unit_values * gain, unit_values, root_factor)


def norm_back(grad_out, unit_values, root_factor, gain):
    scaled = grad_out * gain
    return root_factor * (
        scaled - unit_values * jnp.mean(scaled * unit_values, axis=-1, keepdims=True)
    )


def over_replicas(grad_parts):
    return (
        lax.psum(grad_parts[0].astype(jnp.bfloat16), "rep").astype(jnp.float32),
        lax.psum(grad_parts[1].astype(jnp.bfloat16), "rep").astype(jnp.float32),
    )


def per_device(
    tokens,
    cotangent,
    document_index,
    padding_token_mask,
    attention_gain,
    projection_weight,
    head_gain,
    out_weight,
    feedforward_gain,
    gate_weight,
    up_weight,
    down_weight,
):
    token_rows = tokens.shape[0]
    sequence_length = document_index.shape[0]
    shard_rows = projection_weight.shape[0]
    proj_width = projection_weight.shape[1]
    ff_width = gate_weight.shape[1]
    query_total_width = QUERY_HEADS * HEAD_SIZE
    key_total_width = KEY_VALUE_HEADS * HEAD_SIZE
    query_group_width = QUERY_HEADS // KEY_VALUE_HEADS
    score_scale = HEAD_SIZE ** (-0.5)
    tokens_wide = tokens.astype(jnp.float32)
    root_attn = lax.rsqrt(jnp.mean(tokens_wide * tokens_wide, axis=1, keepdims=True) + norm_epsilon)
    unit_attn = tokens_wide * root_attn
    gain_piece = lax.all_gather(attention_gain, ("seq", "ctx"), axis=0, tiled=True)
    weight_piece = lax.all_gather(projection_weight, ("seq", "ctx"), axis=0, tiled=True)
    columns = unit_attn
    normed = (columns * gain_piece.astype(jnp.float32)).astype(jnp.bfloat16)
    result = (
        jnp.dot(normed, weight_piece, preferred_element_type=jnp.float32),
        gain_piece.astype(jnp.float32),
        normed,
    )
    folded_proj = result
    projected_rows = folded_proj[0]
    gain_attn_full = folded_proj[1]
    normed_attn = folded_proj[2]
    queries_raw = projected_rows[:, :query_total_width].reshape(token_rows, QUERY_HEADS, HEAD_SIZE)
    gate_logits = projected_rows[:, query_total_width : 2 * query_total_width]
    keys_raw = projected_rows[
        :, 2 * query_total_width : 2 * query_total_width + key_total_width
    ].reshape(token_rows, KEY_VALUE_HEADS, HEAD_SIZE)
    values_raw = projected_rows[:, 2 * query_total_width + key_total_width :]
    first_row = lax.axis_index("ctx") * token_rows
    positions = first_row + jnp.arange(token_rows, dtype=jnp.int32)
    cosine_table, sine_table = rope_tables(positions)
    head_gain_wide = head_gain.astype(jnp.float32)
    query_normed, query_unit, query_root = head_norm(queries_raw, head_gain_wide[0])
    key_normed, key_unit, key_root = head_norm(keys_raw, head_gain_wide[1])
    query_low = (
        rotate(query_normed, cosine_table, sine_table)
        .astype(jnp.bfloat16)
        .reshape(token_rows, KEY_VALUE_HEADS, query_group_width, HEAD_SIZE)
    )
    key_low = (
        rotate(key_normed, cosine_table, sine_table)
        .astype(jnp.bfloat16)
        .reshape(token_rows, key_total_width)
    )
    value_low = values_raw.astype(jnp.bfloat16)
    every_key, every_value = (
        lax.all_gather(key_low, "ctx", axis=0, tiled=True),
        lax.all_gather(value_low, "ctx", axis=0, tiled=True),
    )
    every_key = every_key.reshape(sequence_length, KEY_VALUE_HEADS, HEAD_SIZE)
    every_value = every_value.reshape(sequence_length, KEY_VALUE_HEADS, HEAD_SIZE)
    seg_here = lax.dynamic_slice_in_dim(document_index, first_row, token_rows, 0)
    pad_here = lax.dynamic_slice_in_dim(padding_token_mask, first_row, token_rows, 0)
    key_places = jnp.arange(sequence_length, dtype=jnp.int32)
    allowed = (seg_here[:, None] == document_index[None, :]) & (
        key_places[None, :] <= positions[:, None]
    ) & (padding_token_mask[None, :] == 1) | (key_places[None, :] == positions[:, None])

    def masked_scores():
        raw_scores = (
            jnp.einsum("qhgd,khd->hgqk", query_low, every_key, preferred_element_type=jnp.float32)
            * score_scale
        )
        return jnp.where(allowed[None, None], raw_scores, masked_value)

    scores = masked_scores()
    peak = jnp.max(scores, axis=3, keepdims=True)
    exp_scores = jnp.exp(scores - peak)
    denominator = jnp.sum(exp_scores, axis=3, keepdims=True)
    log_total = peak + jnp.log(denominator)
    probs_low = (exp_scores / denominator).astype(jnp.bfloat16)
    attended_rows = jnp.einsum(
        "hgqk,khd->qhgd", probs_low, every_value, preferred_element_type=jnp.float32
    ).reshape(token_rows, query_total_width)
    gate_activations = jax.nn.sigmoid(gate_logits)
    mixed_heads = (attended_rows * gate_activations).astype(jnp.bfloat16)
    columns = lax.dot_general(
        mixed_heads,
        lax.all_gather(out_weight, ("seq", "ctx"), axis=0, tiled=True),
        contract_cols,
        preferred_element_type=jnp.float32,
    )
    result = (columns,)
    folded_out = result
    resid_mid = tokens_wide + folded_out[0]
    root_mlp = lax.rsqrt(jnp.mean(resid_mid * resid_mid, axis=1, keepdims=True) + norm_epsilon)
    unit_mlp = resid_mid * root_mlp
    gain_piece = lax.all_gather(feedforward_gain, ("seq", "ctx"), axis=0, tiled=True)
    gate_piece = lax.all_gather(gate_weight, ("seq", "ctx"), axis=0, tiled=True)
    up_piece = lax.all_gather(up_weight, ("seq", "ctx"), axis=0, tiled=True)
    columns = unit_mlp
    normed = (columns * gain_piece.astype(jnp.float32)).astype(jnp.bfloat16)
    result = (
        jnp.dot(normed, gate_piece, preferred_element_type=jnp.float32),
        jnp.dot(normed, up_piece, preferred_element_type=jnp.float32),
        gain_piece.astype(jnp.float32),
        normed,
    )
    folded_mlp = result
    gate_lin = folded_mlp[0]
    up_lin = folded_mlp[1]
    gain_mlp_full = folded_mlp[2]
    normed_mlp = folded_mlp[3]
    gate_sig = jax.nn.sigmoid(gate_lin)
    silu_gate = gate_lin * gate_sig
    hidden_low = (silu_gate * up_lin).astype(jnp.bfloat16)
    columns = lax.dot_general(
        hidden_low,
        lax.all_gather(down_weight, ("seq", "ctx"), axis=0, tiled=True),
        contract_cols,
        preferred_element_type=jnp.float32,
    )
    result = (columns,)
    layer_out = (resid_mid + result[0]).astype(jnp.bfloat16)
    masked_grad = cotangent.astype(jnp.float32) * pad_here.astype(jnp.float32)[:, None]
    d_out_low = masked_grad.astype(jnp.bfloat16)
    columns = d_out_low
    d_hidden = jnp.dot(
        columns,
        lax.all_gather(down_weight, ("seq", "ctx"), axis=0, tiled=True),
        preferred_element_type=jnp.float32,
    )
    d_gate_low = (d_hidden * up_lin * gate_sig * (1.0 + gate_lin * (1.0 - gate_sig))).astype(
        jnp.bfloat16
    )
    d_up_low = (d_hidden * silu_gate).astype(jnp.bfloat16)
    gate_piece = lax.all_gather(gate_weight, ("seq", "ctx"), axis=0, tiled=True)
    up_piece = lax.all_gather(up_weight, ("seq", "ctx"), axis=0, tiled=True)
    columns = lax.dot_general(
        d_gate_low, gate_piece, contract_cols, preferred_element_type=jnp.float32
    ) + lax.dot_general(d_up_low, up_piece, contract_cols, preferred_element_type=jnp.float32)
    d_normed_mlp = columns
    normed_rows = normed_mlp
    grad_rows = d_out_low
    mlp_grads = lax.psum_scatter(
        jnp.concatenate(
            [
                lax.dot_general(
                    normed_rows, d_gate_low, contract_rows, preferred_element_type=jnp.float32
                ),
                lax.dot_general(
                    normed_rows, d_up_low, contract_rows, preferred_element_type=jnp.float32
                ),
                lax.dot_general(
                    grad_rows, hidden_low, contract_rows, preferred_element_type=jnp.float32
                ),
            ],
            axis=1,
        ).astype(jnp.bfloat16),
        ("seq", "ctx"),
        scatter_dimension=0,
        tiled=True,
    ).astype(jnp.float32)
    gain_mlp_term = jnp.sum(d_normed_mlp * unit_mlp, axis=0)
    d_resid_mid = masked_grad + norm_back(d_normed_mlp, unit_mlp, root_mlp, gain_mlp_full)
    d_attn_low = d_resid_mid.astype(jnp.bfloat16)
    columns = d_attn_low
    mixed_gradient = jnp.dot(
        columns,
        lax.all_gather(out_weight, ("seq", "ctx"), axis=0, tiled=True),
        preferred_element_type=jnp.float32,
    )
    d_gate_logits = mixed_gradient * attended_rows * gate_activations * (1.0 - gate_activations)
    d_attended_low = (
        (mixed_gradient * gate_activations)
        .astype(jnp.bfloat16)
        .reshape(token_rows, KEY_VALUE_HEADS, query_group_width, HEAD_SIZE)
    )
    probs = jnp.exp(masked_scores() - log_total)
    d_probs = jnp.einsum(
        "qhgd,khd->hgqk", d_attended_low, every_value, preferred_element_type=jnp.float32
    )
    value_term = jnp.einsum(
        "hgqk,qhgd->khd", probs_low, d_attended_low, preferred_element_type=jnp.float32
    )
    delta = jnp.sum(probs * d_probs, axis=3, keepdims=True)
    d_scores_low = (probs * (d_probs - delta)).astype(jnp.bfloat16)
    d_queries = (
        jnp.einsum("hgqk,khd->qhgd", d_scores_low, every_key, preferred_element_type=jnp.float32)
        * score_scale
    )
    key_term = (
        jnp.einsum("hgqk,qhgd->khd", d_scores_low, query_low, preferred_element_type=jnp.float32)
        * score_scale
    )
    key_gradient, d_values = (
        lax.psum_scatter(
            key_term.reshape(sequence_length, key_total_width).astype(jnp.bfloat16),
            "ctx",
            scatter_dimension=0,
            tiled=True,
        ).astype(jnp.float32),
        lax.psum_scatter(
            value_term.reshape(sequence_length, key_total_width).astype(jnp.bfloat16),
            "ctx",
            scatter_dimension=0,
            tiled=True,
        ).astype(jnp.float32),
    )
    d_query_normed = inverse_rotation(
        d_queries.reshape(token_rows, QUERY_HEADS, HEAD_SIZE), cosine_table, sine_table
    )
    normed_key_gradient = inverse_rotation(
        key_gradient.reshape(token_rows, KEY_VALUE_HEADS, HEAD_SIZE), cosine_table, sine_table
    )
    head_term = jnp.stack(
        [
            jnp.sum(d_query_normed * query_unit, axis=(0, 1)),
            jnp.sum(normed_key_gradient * key_unit, axis=(0, 1)),
        ]
    )
    d_query_raw = norm_back(d_query_normed, query_unit, query_root, head_gain_wide[0])
    d_key_raw = norm_back(normed_key_gradient, key_unit, key_root, head_gain_wide[1])
    d_proj_low = jnp.concatenate(
        [
            d_query_raw.reshape(token_rows, query_total_width),
            d_gate_logits,
            d_key_raw.reshape(token_rows, key_total_width),
            d_values,
        ],
        axis=1,
    ).astype(jnp.bfloat16)
    columns = lax.dot_general(
        d_proj_low,
        lax.all_gather(projection_weight, ("seq", "ctx"), axis=0, tiled=True),
        contract_cols,
        preferred_element_type=jnp.float32,
    )
    normed_rows = normed_attn
    grad_rows = d_attn_low
    attn_grads = lax.psum_scatter(
        jnp.concatenate(
            [
                lax.dot_general(
                    normed_rows, d_proj_low, contract_rows, preferred_element_type=jnp.float32
                ),
                lax.dot_general(
                    grad_rows, mixed_heads, contract_rows, preferred_element_type=jnp.float32
                ),
            ],
            axis=1,
        ).astype(jnp.bfloat16),
        ("seq", "ctx"),
        scatter_dimension=0,
        tiled=True,
    ).astype(jnp.float32)
    gain_attn_term = jnp.sum(columns * unit_attn, axis=0)
    tokens_grad = (d_resid_mid + norm_back(columns, unit_attn, root_attn, gain_attn_full)).astype(
        jnp.bfloat16
    )
    sum_attn_gain, sum_mlp_gain, sum_head_gain = lax.psum(
        (gain_attn_term, gain_mlp_term, head_term), ("rep", "seq", "ctx")
    )
    mlp_grads, attn_grads = over_replicas((mlp_grads, attn_grads))
    group_rank = lax.axis_index(("seq", "ctx"))
    attention_gain_grad = lax.dynamic_slice_in_dim(
        sum_attn_gain, group_rank * shard_rows, shard_rows, 0
    )
    feedforward_gain_grad = lax.dynamic_slice_in_dim(
        sum_mlp_gain, group_rank * shard_rows, shard_rows, 0
    )
    return (
        layer_out,
        tokens_grad,
        attention_gain_grad,
        attn_grads[:, :proj_width],
        sum_head_gain,
        attn_grads[:, proj_width:],
        feedforward_gain_grad,
        mlp_grads[:, :ff_width],
        mlp_grads[:, ff_width : 2 * ff_width],
        mlp_grads[:, 2 * ff_width :],
    )


def solution(mesh):
    in_specs = (
        P(("rep", "seq", "ctx"), None),
        P(("rep", "seq", "ctx"), None),
        P(("rep", "seq")),
        P(("rep", "seq")),
        P(("seq", "ctx")),
        P(("seq", "ctx"), None),
        P(),
        P(("seq", "ctx"), None),
        P(("seq", "ctx")),
        P(("seq", "ctx"), None),
        P(("seq", "ctx"), None),
        P(("seq", "ctx"), None),
    )
    out_specs = (
        P(("rep", "seq", "ctx"), None),
        P(("rep", "seq", "ctx"), None),
        P(("seq", "ctx")),
        P(("seq", "ctx"), None),
        P(),
        P(("seq", "ctx"), None),
        P(("seq", "ctx")),
        P(("seq", "ctx"), None),
        P(("seq", "ctx"), None),
        P(("seq", "ctx"), None),
    )
    return jax.shard_map(
        per_device, mesh=mesh, in_specs=in_specs, out_specs=out_specs, check_vma=False
    )
```

profile of v0, /device:TPU:0, one launch (start us, length us, event | category | flops | bytes accessed | tf_op | source)
XLA Modules:
  0.0 4382.5 jit_solution(18146430784652032975)
XLA Ops:
  8.0 22.4 all-gather
  30.7 462.0 %all-gather.10.cloned.1.call-done = bf16[2048,6144]{1,0:T(8,128)(2,1)} async-done(((bf16[256,6144]{1,0:T(8,128)(2,1)}), bf16[2048,6144]{1,0:T(8,128)(2,1)}) %all-gather.10.cloned.1.call-update) | async-done | bytes 25165840 | tf_op jit(solution)/shard_map/all_gather | solution.py:98
  492.8 11.7 fusion.46
  504.5 2.7 copy-done.13
  508.8 1.4 slice_bitcast_fusion.1
  516.4 20.9 all-gather.1
  538.3 1.7 slice_bitcast_fusion
  545.0 10.4 all-gather.12.cloned.1.call-done
  555.5 2.2 copy.123
  557.7 45.0 %all-gather.14.cloned.1.call-done = bf16[1024,1024]{0,1:T(8,128)(2,1)} async-done(((bf16[256,1024]{0,1:T(8,128)(2,1)}), bf16[1024,1024]{0,1:T(8,128)(2,1)}) %all-gather.14.cloned.1.call-update) | async-done | bytes 2097168 | tf_op jit(solution)/shard_map/all_gather | solution.py:134
  602.7 12.2 fusion.56
  615.0 8.1 fusion.3
  623.1 7.6 divide_convert_fusion
  630.7 3.2 fusion.27
  634.7 1.9 copy.113
  636.6 3.9 multiply_convert_fusion.6
  640.5 87.4 %all-gather.16.cloned.1.call-done = bf16[2048,2048]{1,0:T(8,128)(2,1)} async-done(((bf16[256,2048]{1,0:T(8,128)(2,1)}), bf16[2048,2048]{1,0:T(8,128)(2,1)}) %all-gather.16.cloned.1.call-update) | async-done | bytes 8388624 | tf_op jit(solution)/shard_map/all_gather | solution.py:166
  727.9 6.2 multiply_reduce_fusion.3
  734.4 473.5 %all-gather.18.cloned.1.call-done = bf16[2048,6144]{1,0:T(8,128)(2,1)} async-done(((bf16[256,6144]{1,0:T(8,128)(2,1)}), bf16[2048,6144]{1,0:T(8,128)(2,1)}) %all-gather.18.cloned.1.call-update) | async-done | bytes 25165840 | tf_op jit(solution)/shard_map/all_gather | solution.py:176
  1207.9 14.3 fusion.57
  1222.2 468.7 %all-gather.20.cloned.1.call-done = bf16[2048,6144]{1,0:T(8,128)(2,1)} async-done(((bf16[256,6144]{1,0:T(8,128)(2,1)}), bf16[2048,6144]{1,0:T(8,128)(2,1)}) %all-gather.20.cloned.1.call-update) | async-done | bytes 25165840 | tf_op jit(solution)/shard_map/all_gather | solution.py:177
  1690.9 14.3 fusion.58
  1705.3 468.9 %all-gather.22.cloned.1.call-done = bf16[2048,6144]{1,0:T(8,128)(2,1)} async-done(((bf16[256,6144]{1,0:T(8,128)(2,1)}), bf16[2048,6144]{1,0:T(8,128)(2,1)}) %all-gather.22.cloned.1.call-update) | async-done | bytes 25165840 | tf_op jit(solution)/shard_map/all_gather | solution.py:196
  2174.1 19.1 multiply_convert_fusion
  2193.2 13.5 fusion.59
  2206.7 15.2 multiply_reduce_fusion
  2221.9 2.4 multiply_add_fusion.1
  2224.4 8.6 multiply_convert_fusion.3
  2234.1 14.6 fusion
  2251.1 10.1 fusion.2
  2261.3 7.7 fusion.5
  2270.3 7.5 bitcast_convert_fusion
  2277.8 4.1 copy.117
  2282.0 4.7 convolution_multiply_fusion
  2287.9 2.6 copy.119
  2290.5 2.5 copy.118
  2293.0 2.2 multiply_add_fusion
  2295.2 2.1 multiply_reduce_fusion.1
  2298.6 4.8 fusion.22
  2303.4 5.7 convolution_convert_fusion.4
  2309.1 5.0 reduce-scatter.5.cloned.1.call-done
  2314.1 1.9 fusion.55
  2316.4 2.5 copy.120
  2318.9 1.4 multiply_add_fusion.2
  2320.4 1.6 multiply_reduce_fusion.5
  2322.7 2.7 fusion.34
  2325.4 34.5 reduce-scatter.7.cloned.1.call-done
  2359.9 12.6 convolution_convert_fusion.3
  2372.5 22.9 pad_maximum_fusion.1
  2396.6 13.9 convolution_convert_fusion.1
  2410.5 14.0 convolution_convert_fusion.2
  2424.5 14.2 convolution_convert_fusion
  2438.7 50.8 %pad_maximum_fusion = bf16[2048,18432]{1,0:T(8,128)(2,1)} fusion(bf16[2048,6144]{1,0:T(8,128)(2,1)} %convolution_convert_fusion, bf16[2048,6144]{1,0:T(8,128)(2,1)} %convolution_convert_fusion.1, bf16[2048,6144]{1,0:T(8,128)(2,1)} %convolution_convert_fusion.2), kind=kLoop, calls=%fused_computation | loop fusion | flops 226492416 | bytes 150994944 | tf_op jit(solution)/shard_map/concatenate | solution.py:223
  2489.5 448.2 %reduce-scatter.9.cloned.1.call-done = bf16[256,8192]{1,0:T(8,128)(2,1)} async-done(((bf16[2048,8192]{1,0:T(8,128)(2,1)}), bf16[256,8192]{1,0:T(8,128)(2,1)}) %reduce-scatter.9.cloned.1.call-update) | async-done | bytes 4194320 | tf_op jit(solution)/shard_map/reduce_scatter | solution.py:318
  2937.7 1180.7 %reduce-scatter.11.cloned.1.call-done = bf16[256,18432]{1,0:T(8,128)(2,1)} async-done(((bf16[2048,18432]{1,0:T(8,128)(2,1)}), bf16[256,18432]{1,0:T(8,128)(2,1)}) %reduce-scatter.11.cloned.1.call-update) | async-done | bytes 9437200 | tf_op jit(solution)/shard_map/reduce_scatter | solution.py:222
  4118.5 1.5 copy-done.20
  4120.0 15.0 fusion.10
  4135.1 14.9 fusion.17
  4150.0 40.8 all-reduce
  4192.0 3.2 fusion.16
  4195.1 164.5 %all-reduce.4.cloned.1.call-done = (bf16[256,8192]{1,0:T(8,128)(2,1)}, bf16[256,18432]{1,0:T(8,128)(2,1)}) async-done(((bf16[256,8192]{1,0:T(8,128)(2,1)}, bf16[256,18432]{1,0:T(8,128)(2,1)}), (bf16[256,8192]{1,0:T(8,128)(2,1)}, bf16[256,18432]{1,0:T(8,128)(2,1)})) %all-reduce.4.cloned.1.call-update) | async-done | bytes 13631504 | tf_op jit(solution)/shard_map/psum | solution.py:67
  4359.7 5.9 slice.91
  4365.6 2.8 slice.92
  4368.4 6.9 fusion.53
  (197 shorter events, 26.6 us)
Async XLA Ops:
  7.2 23.2 copy-start.16
  7.2 485.6 %all-gather.10.cloned.1.call-start = ((), (), s32[]{:S(2)}) async-start(), calls=%async_computation.4 | async-start | bytes 28311552 | tf_op jit(solution)/shard_map/all_gather | solution.py:98
  7.9 547.5 %all-gather.12.cloned.1.call-start = ((), (), s32[]{:S(2)}) async-start(), calls=%async_computation.5 | async-start | bytes 2621440 | tf_op jit(solution)/shard_map/all_gather | solution.py:135
  30.4 474.1 %copy-start.36 = (f32[8,1,256]{2,1,0:T(1,128)}, f32[8,1,256]{2,1,0:T(1,128)S(1)}, u32[]{:S(2)}) copy-start(f32[8,1,256]{2,1,0:T(1,128)S(1)} %convert_element_type.136) | copy-start | bytes 24580
  30.7 473.8 %copy-start.38 = (f32[256]{0:T(256)}, f32[256]{0:T(256)S(1)}, u32[]{:S(2)}) copy-start(f32[256]{0:T(256)S(1)} %add_rsqrt_fusion.3) | copy-start | bytes 3076
  492.8 15.4 copy-start.55
  504.5 2.7 copy-start.13
  508.1 94.6 %all-gather.14.cloned.1.call-start = ((), (), s32[]{:S(2)}) async-start(), calls=%async_computation.6 | async-start | bytes 2621440 | tf_op jit(solution)/shard_map/all_gather | solution.py:134
  508.2 3.6 copy-start.47
  508.2 32.9 copy-start.49
  508.8 33.9 copy-start.27
  508.8 33.9 copy-start.29
  513.8 214.1 %all-gather.16.cloned.1.call-start = ((), (), s32[]{:S(2)}) async-start(), calls=%async_computation.7 | async-start | bytes 9437184 | tf_op jit(solution)/shard_map/all_gather | solution.py:166
  514.4 693.5 %all-gather.18.cloned.1.call-start = ((), (), s32[]{:S(2)}) async-start(), calls=%async_computation.8 | async-start | bytes 28311552 | tf_op jit(solution)/shard_map/all_gather | solution.py:176
  515.0 22.3 copy-start.52
  515.0 22.4 copy-start.53
  515.0 1175.9 %all-gather.20.cloned.1.call-start = ((), (), s32[]{:S(2)}) async-start(), calls=%async_computation.9 | async-start | bytes 28311552 | tf_op jit(solution)/shard_map/all_gather | solution.py:177
  515.6 1658.5 %all-gather.22.cloned.1.call-start = ((), (), s32[]{:S(2)}) async-start(), calls=%async_computation.10 | async-start | bytes 28311552 | tf_op jit(solution)/shard_map/all_gather | solution.py:196
  516.3 1797.7 %reduce-scatter.5.cloned.1.call-start = ((), (), s32[]{:S(2)}) async-start(), calls=%async_computation.11 | async-start | bytes 2621440 | tf_op jit(solution)/shard_map/reduce_scatter | solution.py:274
  541.1 2.4 copy-start.32
  543.7 59.0 %copy-start.14 = (bf16[256,16,64]{2,0,1:T(8,128)(2,1)}, bf16[256,16,64]{2,0,1:T(8,128)(2,1)S(1)}, u32[]{:S(2)}) copy-start(bf16[256,16,64]{2,0,1:T(8,128)(2,1)S(1)} %copy.80) | copy-start | bytes 1572868
  557.7 73.0 %copy-start.7 = (bf16[128,8,8,128]{3,2,1,0:T(8,128)(2,1)}, bf16[128,8,8,128]{3,2,1,0:T(8,128)(2,1)S(1)}, u32[]{:S(2)}) copy-start(bf16[128,8,8,128]{3,2,1,0:T(8,128)(2,1)S(1)} %copy.123) | copy-start | bytes 6291460
  615.0 8.1 copy-start.40
  623.1 7.7 copy-start.42
  630.7 4.0 copy-start
  636.6 3.9 copy-start.21
  636.6 91.3 %copy-start.17 = (bf16[256,2048]{1,0:T(8,128)(2,1)S(1)}, bf16[256,2048]{1,0:T(8,128)(2,1)}, u32[]{:S(2)}) copy-start(bf16[256,2048]{1,0:T(8,128)(2,1)} %param.12) | copy-start | bytes 3145732
  734.1 1487.8 %copy-start.19 = (f32[256,2048]{1,0:T(8,128)}, f32[256,2048]{1,0:T(8,128)S(1)}, u32[]{:S(2)}) copy-start(f32[256,2048]{1,0:T(8,128)S(1)} %get-tuple-element.54) | copy-start | bytes 6291460
  734.4 956.6 %copy-start.11 = (bf16[256,2048]{1,0:T(8,128)(2,1)}, bf16[256,2048]{1,0:T(8,128)(2,1)S(1)}, u32[]{:S(2)}) copy-start(bf16[256,2048]{1,0:T(8,128)(2,1)S(1)} %multiply_convert_fusion.5) | copy-start | bytes 3145732
  2206.7 15.2 copy-start.23
  2221.9 2.4 copy-start.22
  2224.3 8.6 copy-start.4
  2224.3 9.1 copy-start.41
  2224.3 9.1 copy-start.43
  2234.1 14.7 slice-start
  2234.1 14.7 slice-start.1
  2234.1 15.9 slice-start.2
  2234.1 17.1 slice-start.3
  2251.1 10.1 copy-start.15
  2261.3 7.8 copy-start.48
  2261.3 8.4 copy-start.50
  2269.0 90.8 %reduce-scatter.7.cloned.1.call-start = ((), (), s32[]{:S(2)}) async-start(), calls=%async_computation.12 | async-start | bytes 2621440 | tf_op jit(solution)/shard_map/reduce_scatter | solution.py:280
  2277.8 4.2 copy-start.8
  2281.9 655.8 %reduce-scatter.9.cloned.1.call-start = ((), (), s32[]{:S(2)}) async-start(), calls=%async_computation.13 | async-start | bytes 37748736 | tf_op jit(solution)/shard_map/reduce_scatter | solution.py:318
  2287.9 5.1 copy-start.28
  2287.9 5.1 copy-start.30
  2292.9 2.3 copy-start.33
  2298.5 4.8 copy-start.5
  2298.6 4.8 copy-start.26
  2303.4 56.5 %copy-start.25 = (bf16[256,2048]{1,0:T(8,128)(2,1)}, bf16[256,2048]{1,0:T(8,128)(2,1)S(1)}, u32[]{:S(2)}) copy-start(bf16[256,2048]{1,0:T(8,128)(2,1)S(1)} %get-tuple-element.27) | copy-start | bytes 3145732
  2316.4 3.9 copy-start.10
  2316.4 3.9 copy-start.35
  2320.3 2.3 copy-start.46
  2322.3 37.6 copy-start.18
  2322.3 37.6 copy-start.37
  2322.3 37.6 copy-start.39
  2325.3 47.1 %copy-start.31 = (bf16[256,1024]{1,0:T(8,128)(2,1)}, bf16[256,1024]{1,0:T(8,128)(2,1)S(1)}, u32[]{:S(2)}) copy-start(bf16[256,1024]{1,0:T(8,128)(2,1)S(1)} %get-tuple-element.32) | copy-start | bytes 1572868
  2395.4 1723.1 %reduce-scatter.11.cloned.1.call-start = ((), (), s32[]{:S(2)}) async-start(), calls=%async_computation.14 | async-start | bytes 84934656 | tf_op jit(solution)/shard_map/reduce_scatter | solution.py:222
  2410.5 14.0 copy-start.24
  2489.5 1870.2 %all-reduce.4.cloned.1.call-start = ((), (), s32[]{:S(2)}) async-start(), calls=%async_computation.15 | async-start | bytes 27262976 | tf_op jit(solution)/shard_map/psum | solution.py:67
  4120.0 15.0 copy-start.45
  4135.1 14.9 copy-start.51
  4135.1 56.9 %copy-start.6 = (f32[256,2048]{1,0:T(8,128)S(1)}, f32[256,2048]{1,0:T(8,128)}, u32[]{:S(2)}) copy-start(f32[256,2048]{1,0:T(8,128)} %copy-done.4) | copy-start | bytes 6291460
  4359.7 8.7 copy-start.1
  (9 other events, 12.0 us)
Sparse Core Ops, SparseCore 0:
  9.6 483.1 all-gather.9
  508.2 47.1 all-gather.11
  557.6 45.0 all-gather.13
  604.7 123.1 all-gather.15
  729.3 478.5 all-gather.17
  1209.3 481.6 all-gather.19
  1692.5 481.6 all-gather.21
  2269.1 44.8 reduce-scatter.4
  2316.5 43.3 reduce-scatter.6
  2395.5 542.1 reduce-scatter.8
  2941.6 1176.8 reduce-scatter.10
  4121.1 238.5 all-reduce.3
where the time goes:
time: 4390 us; the launch traced here: 4380 us
  waiting for transfers between devices  3850 us (88%)
  matrix products  243 us (6%)
  other arithmetic  130 us (3%)
  blocking collectives  84 us (2%)
  local copies, waits for them, and re-layouts  57.2 us (1%)
    reduce_scatter x1, waiting for transfers between devices, per_device(): lax.psum_scatter(jnp.concatenate([lax.dot_general(normed_rows, d_gate_low...  1180 us
    all_gather x1, waiting for transfers between devices, per_device(): gate_piece = lax.all_gather(gate_weight, ('seq', 'ctx'), axis=0, tiled=True)  474 us
    all_gather x1, waiting for transfers between devices, per_device(): lax.all_gather(down_weight, ('seq', 'ctx'), axis=0, tiled=True)  469 us
    all_gather x1, waiting for transfers between devices, per_device(): up_piece = lax.all_gather(up_weight, ('seq', 'ctx'), axis=0, tiled=True)  469 us
    all_gather x1, waiting for transfers between devices, per_device(): lax.all_gather(projection_weight, ('seq', 'ctx'), axis=0, tiled=True)  462 us
    reduce_scatter x1, waiting for transfers between devices, per_device(): lax.psum_scatter(jnp.concatenate([lax.dot_general(normed_rows, d_proj_low...  448 us
    psum x1, waiting for transfers between devices, over_replicas(): lax.psum(grad_parts[1].astype(jnp.bfloat16), 'rep').astype(jnp.float32)  165 us
  transfers between devices with their start and end apart: 12, of which 12 were waited for; matrix products, arithmetic and copies ran while one was open for 6% of the time, Pallas kernels for 0%

commit v1 on v0

--- a/solution.py
+++ b/solution.py
@@ -11,6 +11,19 @@
 masked_value = -1e30
 contract_rows = (((0,), (0,)), ((), ()))
 contract_cols = (((1,), (1,)), ((), ()))
+
+
+def ring_gather(shard, axis, dim):
+    ways = lax.axis_size(axis)
+    up = [(d, (d + 1) % ways) for d in range(ways)]
+    down = [(d, (d - 1) % ways) for d in range(ways)]
+    earlier, later = ([shard], [shard])
+    for _ in range(ways // 2):
+        earlier.append(lax.ppermute(earlier[-1], axis, up))
+    for _ in range((ways - 1) // 2):
+        later.append(lax.ppermute(later[-1], axis, down))
+    line = jnp.concatenate([*earlier[::-1], *later[1:]], axis=dim)
+    return jnp.roll(line, (lax.axis_index(axis) - ways // 2) * shard.shape[dim], axis=dim)
 
 
 def rope_tables(positions):
@@ -173,7 +186,7 @@
     root_mlp = lax.rsqrt(jnp.mean(resid_mid * resid_mid, axis=1, keepdims=True) + norm_epsilon)
     unit_mlp = resid_mid * root_mlp
     gain_piece = lax.all_gather(feedforward_gain, ("seq", "ctx"), axis=0, tiled=True)
-    gate_piece = lax.all_gather(gate_weight, ("seq", "ctx"), axis=0, tiled=True)
+    gate_piece = ring_gather(gate_weight, ("seq", "ctx"), 0)
     up_piece = lax.all_gather(up_weight, ("seq", "ctx"), axis=0, tiled=True)
     columns = unit_mlp
     normed = (columns * gain_piece.astype(jnp.float32)).astype(jnp.bfloat16)

time: 4390 us -> 4820 us (1.098)
  starting transfers between devices: 0.48 us -> 318 us
  blocking collectives: 84 us -> 200 us
  waiting for transfers between devices: 3850 us -> 3800 us
  local copies, waits for them, and re-layouts: 57.2 us -> 106 us
    ppermute x0 -> x7, waiting for transfers between devices: none -> 489 us  [the longest x4 412 us: ring_gather(): earlier.append(lax.ppermute(earlier[-1], axis, up))]
    all_gather x1, waiting for transfers between devices: 469 us -> 0.01 us  [per_device(): lax.all_gather(down_weight, ('seq', 'ctx'), axis=0, tiled=True)]
    ppermute x0 -> x7, starting transfers between devices: none -> 317 us  [the longest x4 311 us: ring_gather(): earlier.append(lax.ppermute(earlier[-1], axis, up))]
    all_gather x1, blocking collectives: 20.9 us -> 136 us  [per_device(): lax.all_gather(feedforward_gain, ('seq', 'ctx'), axis=0, tiled=True)]
  transfers between devices with their start and end apart: 12 -> 19, of which waited for: 12 -> 14; matrix products, arithmetic and copies ran while one was open for 6% -> 7% of each run, Pallas kernels for 0% -> 0%
where the time goes in v1:
time: 4820 us; the launch traced here: 4810 us
  waiting for transfers between devices  3800 us (79%)
  starting transfers between devices  318 us (7%)
  matrix products  243 us (5%)
  blocking collectives  200 us (4%)
  other arithmetic  131 us (3%)
  local copies, waits for them, and re-layouts  106 us (2%)
    reduce_scatter x1, waiting for transfers between devices, per_device(): lax.psum_scatter(jnp.concatenate([lax.dot_general(normed_rows, d_gate_low...  1180 us
    all_gather x1, waiting for transfers between devices, per_device(): up_piece = lax.all_gather(up_weight, ('seq', 'ctx'), axis=0, tiled=True)  474 us
    all_gather x1, waiting for transfers between devices, per_device(): lax.all_gather(projection_weight, ('seq', 'ctx'), axis=0, tiled=True)  461 us
    all_gather x1, waiting for transfers between devices, per_device(): gate_piece = lax.all_gather(gate_weight, ('seq', 'ctx'), axis=0, tiled=True)  450 us
    reduce_scatter x1, waiting for transfers between devices, per_device(): lax.psum_scatter(jnp.concatenate([lax.dot_general(normed_rows, d_proj_low...  449 us
    ppermute x4, waiting for transfers between devices, ring_gather(): earlier.append(lax.ppermute(earlier[-1], axis, up))  412 us
    ppermute x4, starting transfers between devices, ring_gather(): earlier.append(lax.ppermute(earlier[-1], axis, up))  311 us
    psum x1, waiting for transfers between devices, over_replicas(): lax.psum(grad_parts[1].astype(jnp.bfloat16), 'rep').astype(jnp.float32)  165 us
  transfers between devices with their start and end apart: 19, of which 14 were waited for; matrix products, arithmetic and copies ran while one was open for 7% of the time, Pallas kernels for 0%

profile of v1, /device:TPU:0, one launch (start us, length us, event | category | flops | bytes accessed | tf_op | source)
XLA Modules:
  0.0 4809.9 jit_solution(17004080988189481351)
XLA Ops:
  8.8 22.5 all-gather
  31.6 461.2 %all-gather.10.cloned.1.call-done = bf16[2048,6144]{1,0:T(8,128)(2,1)} async-done(((bf16[256,6144]{1,0:T(8,128)(2,1)}), bf16[2048,6144]{1,0:T(8,128)(2,1)}) %all-gather.10.cloned.1.call-update) | async-done | bytes 25165840 | tf_op jit(solution)/shard_map/all_gather | solution.py:111
  492.8 11.7 fusion.48
  504.5 2.7 copy-done.14
  517.8 139.2 %collective-permute-done = bf16[256,6144]{1,0:T(8,128)(2,1)S(1)} collective-permute-done((bf16[256,6144]{1,0:T(8,128)(2,1)S(1)}, bf16[256,6144]{1,0:T(8,128)(2,1)S(1)}, u32[]{:S(2)}, u32[]{:S(2)}) %collective-permute-start) | collective-permute-done | bytes 3145760 | tf_op jit(solution)/shard_map/ppermute | solution.py:22
  657.0 61.0 %collective-permute-start.1 = (bf16[256,6144]{1,0:T(8,128)(2,1)S(1)}, bf16[256,6144]{1,0:T(8,128)(2,1)S(1)}, u32[]{:S(2)}, u32[]{:S(2)}) collective-permute-start(bf16[256,6144]{1,0:T(8,128)(2,1)S(1)} %collective-permute-done), channel_id=1, source_target_pairs={{0,1},{1,2},{2,3},{3,4},{4,5},{5,6},{6,7},{7,0},{8,9},{9,10},{10,1... | collective-permute-start | bytes 9437192 | tf_op jit(solution)/shard_map/ppermute | solution.py:22
  719.8 136.3 %collective-permute-done.1 = bf16[256,6144]{1,0:T(8,128)(2,1)S(1)} collective-permute-done((bf16[256,6144]{1,0:T(8,128)(2,1)S(1)}, bf16[256,6144]{1,0:T(8,128)(2,1)S(1)}, u32[]{:S(2)}, u32[]{:S(2)}) %collective-permute-start.1) | collective-permute-done | bytes 3145760 | tf_op jit(solution)/shard_map/ppermute | solution.py:22
  856.1 123.3 %collective-permute-start.2 = (bf16[256,6144]{1,0:T(8,128)(2,1)S(1)}, bf16[256,6144]{1,0:T(8,128)(2,1)}, u32[]{:S(2)}, u32[]{:S(2)}) collective-permute-start(bf16[256,6144]{1,0:T(8,128)(2,1)S(1)} %collective-permute-done.1), channel_id=1, source_target_pairs={{0,1},{1,2},{2,3},{3,4},{4,5},{5,6},{6,7},{7,0},{8,9},{9,10},{10,1... | collective-permute-start | bytes 9437192 | tf_op jit(solution)/shard_map/ppermute | solution.py:22
  979.3 13.0 collective-permute-done.4
  994.6 136.4 %collective-permute-done.2 = bf16[256,6144]{1,0:T(8,128)(2,1)} collective-permute-done((bf16[256,6144]{1,0:T(8,128)(2,1)S(1)}, bf16[256,6144]{1,0:T(8,128)(2,1)}, u32[]{:S(2)}, u32[]{:S(2)}) %collective-permute-start.2) | collective-permute-done | bytes 3145760 | tf_op jit(solution)/shard_map/ppermute | solution.py:22
  1130.9 125.6 %collective-permute-start.3 = (bf16[256,6144]{1,0:T(8,128)(2,1)}, bf16[256,6144]{1,0:T(8,128)(2,1)}, u32[]{:S(2)}, u32[]{:S(2)}) collective-permute-start(bf16[256,6144]{1,0:T(8,128)(2,1)} %collective-permute-done.2), channel_id=1, source_target_pairs={{0,1},{1,2},{2,3},{3,4},{4,5},{5,6},{6,7},{7,0},{8,9},{9,10},{10,1... | collective-permute-start | bytes 9437192 | tf_op jit(solution)/shard_map/ppermute | solution.py:22
  1256.5 136.3 %all-gather.1 = bf16[8,1,256]{2,1,0:T(2,128)(2,1)S(1)} all-gather(bf16[1,1,256]{2,1,0:T(2,128)(2,1)S(1)} %reshape.310), channel_id=1, replica_groups=mesh['rep'=4,'seq'=2,'ctx'=4] {'seq','ctx'}, dimensions={0}, use_global_device_ids=true | all-gather | bytes 4608 | tf_op jit(solution)/shard_map/all_gather | solution.py:188
  1396.3 3.9 constant_dynamic-update-slice_fusion.15
  1400.2 4.1 constant_dynamic-update-slice_fusion.14
  1411.2 3.9 constant_dynamic-update-slice_fusion.10
  1415.0 3.9 constant_dynamic-update-slice_fusion.9
  1418.9 64.2 %collective-permute-done.6 = bf16[256,6144]{1,0:T(8,128)(2,1)S(1)} collective-permute-done((bf16[256,6144]{1,0:T(8,128)(2,1)}, bf16[256,6144]{1,0:T(8,128)(2,1)S(1)}, u32[]{:S(2)}, u32[]{:S(2)}) %collective-permute-start.6) | collective-permute-done | bytes 3145760 | tf_op jit(solution)/shard_map/ppermute | solution.py:24
  1485.2 3.9 constant_dynamic-update-slice_fusion.7
  1489.0 3.9 constant_dynamic-update-slice_fusion.6
  1498.7 3.9 constant_dynamic-update-slice_fusion.2
  1502.6 3.9 constant_dynamic-update-slice_fusion.1
  1515.3 14.5 fusion.45
  1532.1 12.8 fusion.59
  1544.9 8.1 fusion.5
  1553.1 7.6 divide_convert_fusion
  1560.7 3.3 fusion.29
  1566.6 3.9 multiply_convert_fusion.6
  1570.5 86.3 %all-gather.16.cloned.1.call-done = bf16[2048,2048]{1,0:T(8,128)(2,1)} async-done(((bf16[256,2048]{1,0:T(8,128)(2,1)}), bf16[2048,2048]{1,0:T(8,128)(2,1)}) %all-gather.16.cloned.1.call-update) | async-done | bytes 8388624 | tf_op jit(solution)/shard_map/all_gather | solution.py:179
  1656.8 6.2 multiply_reduce_fusion.3
  1663.3 473.5 %all-gather.18.cloned.1.call-done = bf16[2048,6144]{1,0:T(8,128)(2,1)} async-done(((bf16[256,6144]{1,0:T(8,128)(2,1)}), bf16[2048,6144]{1,0:T(8,128)(2,1)}) %all-gather.18.cloned.1.call-update) | async-done | bytes 25165840 | tf_op jit(solution)/shard_map/all_gather | solution.py:190
  2136.8 11.6 fusion.60
  2148.5 21.2 multiply_convert_fusion
  2169.7 450.3 %all-gather.22.cloned.1.call-done = bf16[2048,6144]{1,0:T(8,128)(2,1)} async-done(((bf16[256,6144]{1,0:T(8,128)(2,1)}), bf16[2048,6144]{1,0:T(8,128)(2,1)}) %all-gather.22.cloned.1.call-update) | async-done | bytes 25165840 | tf_op jit(solution)/shard_map/all_gather | solution.py:227
  2620.0 13.6 fusion.61
  2633.7 14.9 multiply_reduce_fusion
  2651.0 8.5 multiply_convert_fusion.3
  2660.7 14.6 fusion.2
  2677.7 10.3 fusion.4
  2688.0 7.7 fusion.7
  2697.0 7.5 bitcast_convert_fusion
  2704.5 4.1 copy.117
  2708.7 4.7 convolution_multiply_fusion
  2714.6 2.6 copy.119
  2725.5 4.8 fusion.24
  2730.3 5.6 convolution_convert_fusion.4
  2736.0 5.0 reduce-scatter.5.cloned.1.call-done
  2749.5 2.7 fusion.36
  2752.2 34.3 reduce-scatter.7.cloned.1.call-done
  2786.5 12.6 convolution_convert_fusion.3
  2799.1 22.8 pad_maximum_fusion.1
  2823.2 13.9 convolution_convert_fusion.1
  2837.1 14.0 convolution_convert_fusion.2
  2851.1 14.2 convolution_convert_fusion
  2865.2 50.8 %pad_maximum_fusion = bf16[2048,18432]{1,0:T(8,128)(2,1)} fusion(bf16[2048,6144]{1,0:T(8,128)(2,1)} %convolution_convert_fusion, bf16[2048,6144]{1,0:T(8,128)(2,1)} %convolution_convert_fusion.1, bf16[2048,6144]{1,0:T(8,128)(2,1)} %convolution_convert_fusion.2), kind=kLoop, calls=%fused_computation | loop fusion | flops 226492416 | bytes 150994944 | tf_op jit(solution)/shard_map/concatenate | solution.py:236
  2916.1 448.7 %reduce-scatter.9.cloned.1.call-done = bf16[256,8192]{1,0:T(8,128)(2,1)} async-done(((bf16[2048,8192]{1,0:T(8,128)(2,1)}), bf16[256,8192]{1,0:T(8,128)(2,1)}) %reduce-scatter.9.cloned.1.call-update) | async-done | bytes 4194320 | tf_op jit(solution)/shard_map/reduce_scatter | solution.py:331
  3364.8 1181.3 %reduce-scatter.11.cloned.1.call-done = bf16[256,18432]{1,0:T(8,128)(2,1)} async-done(((bf16[2048,18432]{1,0:T(8,128)(2,1)}), bf16[256,18432]{1,0:T(8,128)(2,1)}) %reduce-scatter.11.cloned.1.call-update) | async-done | bytes 9437200 | tf_op jit(solution)/shard_map/reduce_scatter | solution.py:235
  4547.6 14.9 fusion.12
  4562.6 14.9 fusion.19
  4577.5 40.7 all-reduce
  4619.6 3.2 fusion.18
  4622.7 164.6 %all-reduce.4.cloned.1.call-done = (bf16[256,8192]{1,0:T(8,128)(2,1)}, bf16[256,18432]{1,0:T(8,128)(2,1)}) async-done(((bf16[256,8192]{1,0:T(8,128)(2,1)}, bf16[256,18432]{1,0:T(8,128)(2,1)}), (bf16[256,8192]{1,0:T(8,128)(2,1)}, bf16[256,18432]{1,0:T(8,128)(2,1)})) %all-reduce.4.cloned.1.call-update) | async-done | bytes 13631504 | tf_op jit(solution)/shard_map/psum | solution.py:80
  4787.3 5.9 slice.91
  4793.2 2.8 slice.92
  4796.0 6.9 fusion.56
  (241 shorter events, 77.7 us)
Async XLA Ops:
  7.2 24.1 copy-start.21
  7.2 485.6 %all-gather.10.cloned.1.call-start = ((), (), s32[]{:S(2)}) async-start(), calls=%async_computation.4 | async-start | bytes 28311552 | tf_op jit(solution)/shard_map/all_gather | solution.py:111
  7.9 1507.4 %all-gather.20.cloned.1.call-start = ((), (), s32[]{:S(2)}) async-start(), calls=%async_computation.9 | async-start | bytes 28311552 | tf_op jit(solution)/shard_map/all_gather | solution.py:209
  8.7 1521.1 %all-gather.12.cloned.1.call-start = ((), (), s32[]{:S(2)}) async-start(), calls=%async_computation.5 | async-start | bytes 2621440 | tf_op jit(solution)/shard_map/all_gather | solution.py:148
  31.3 473.2 %copy-start.43 = (f32[8,1,256]{2,1,0:T(1,128)}, f32[8,1,256]{2,1,0:T(1,128)S(1)}, u32[]{:S(2)}) copy-start(f32[8,1,256]{2,1,0:T(1,128)S(1)} %convert_element_type.136) | copy-start | bytes 24580
  31.6 472.9 %copy-start.45 = (f32[256]{0:T(256)}, f32[256]{0:T(256)S(1)}, u32[]{:S(2)}) copy-start(f32[256]{0:T(256)S(1)} %add_rsqrt_fusion.3) | copy-start | bytes 3076
  492.8 15.4 copy-start.62
  508.1 1024.0 %all-gather.14.cloned.1.call-start = ((), (), s32[]{:S(2)}) async-start(), calls=%async_computation.6 | async-start | bytes 2621440 | tf_op jit(solution)/shard_map/all_gather | solution.py:147
  508.3 1003.1 %copy-start.56 = (f32[128]{0:T(128)}, f32[128]{0:T(128)S(1)}, u32[]{:S(2)}) copy-start(f32[128]{0:T(128)S(1)} %get-tuple-element.49) | copy-start | bytes 1540
  508.8 1004.1 %copy-start.33 = (f32[256,64]{1,0:T(8,128)}, f32[256,64]{1,0:T(8,128)S(1)}, u32[]{:S(2)}) copy-start(f32[256,64]{1,0:T(8,128)S(1)} %get-tuple-element.47) | copy-start | bytes 196612
  508.8 1004.1 %copy-start.35 = (f32[256,64]{1,0:T(8,128)}, f32[256,64]{1,0:T(8,128)S(1)}, u32[]{:S(2)}) copy-start(f32[256,64]{1,0:T(8,128)S(1)} %get-tuple-element.48) | copy-start | bytes 196612
  513.8 1143.0 %all-gather.16.cloned.1.call-start = ((), (), s32[]{:S(2)}) async-start(), calls=%async_computation.7 | async-start | bytes 9437184 | tf_op jit(solution)/shard_map/all_gather | solution.py:179
  514.4 742.1 %copy-start.63 = (bf16[256]{0:T(256)(128)(2,1)S(1)}, bf16[256]{0:T(256)(128)(2,1)}, u32[]{:S(2)}) copy-start(bf16[256]{0:T(256)(128)(2,1)} %param.20) | copy-start | bytes 1540
  514.4 878.5 %copy-start.59 = (s32[1024]{0:T(1024)S(1)}, s32[1024]{0:T(1024)}, u32[]{:S(2)}) copy-start(s32[1024]{0:T(1024)} %param.14) | copy-start | bytes 12292
  514.4 878.5 %copy-start.60 = (s32[1024]{0:T(1024)S(1)}, s32[1024]{0:T(1024)}, u32[]{:S(2)}) copy-start(s32[1024]{0:T(1024)} %param.15) | copy-start | bytes 12292
  514.4 1622.4 %all-gather.18.cloned.1.call-start = ((), (), s32[]{:S(2)}) async-start(), calls=%async_computation.8 | async-start | bytes 28311552 | tf_op jit(solution)/shard_map/all_gather | solution.py:190
  515.0 2105.0 %all-gather.22.cloned.1.call-start = ((), (), s32[]{:S(2)}) async-start(), calls=%async_computation.10 | async-start | bytes 28311552 | tf_op jit(solution)/shard_map/all_gather | solution.py:227
  515.8 2225.2 %reduce-scatter.5.cloned.1.call-start = ((), (), s32[]{:S(2)}) async-start(), calls=%async_computation.11 | async-start | bytes 2621440 | tf_op jit(solution)/shard_map/reduce_scatter | solution.py:287
  516.3 140.7 %collective-permute-start = (bf16[256,6144]{1,0:T(8,128)(2,1)S(1)}, bf16[256,6144]{1,0:T(8,128)(2,1)S(1)}, u32[]{:S(2)}, u32[]{:S(2)}) collective-permute-start(bf16[256,6144]{1,0:T(8,128)(2,1)S(1)} %copy-done.4), channel_id=1, source_target_pairs={{0,1},{1,2},{2,3},{3,4},{4,5},{5,6},{6,7},{7,0},{8,9},{9,10},{10,1... | collective-permute-start | bytes 9437192 | tf_op jit(solution)/shard_map/ppermute | solution.py:22
  657.0 335.3 %copy-start.15 = (bf16[256,6144]{1,0:T(8,128)(2,1)}, bf16[256,6144]{1,0:T(8,128)(2,1)S(1)}, u32[]{:S(2)}) copy-start(bf16[256,6144]{1,0:T(8,128)(2,1)S(1)} %collective-permute-done) | copy-start | bytes 9437188
  657.0 199.1 %collective-permute-start.1 = (bf16[256,6144]{1,0:T(8,128)(2,1)S(1)}, bf16[256,6144]{1,0:T(8,128)(2,1)S(1)}, u32[]{:S(2)}, u32[]{:S(2)}) collective-permute-start(bf16[256,6144]{1,0:T(8,128)(2,1)S(1)} %collective-permute-done), channel_id=1, source_target_pairs={{0,1},{1,2},{2,3},{3,4},{4,5},{5,6},{6,7},{7,0},{8,9},{9,10},{10,1... | collective-permute-start | bytes 9437192 | tf_op jit(solution)/shard_map/ppermute | solution.py:22
  717.9 274.4 %collective-permute-start.4 = (bf16[256,6144]{1,0:T(8,128)(2,1)S(1)}, bf16[256,6144]{1,0:T(8,128)(2,1)}, u32[]{:S(2)}, u32[]{:S(2)}) collective-permute-start(bf16[256,6144]{1,0:T(8,128)(2,1)S(1)} %copy-done.4), channel_id=1, source_target_pairs={{0,7},{1,0},{2,1},{3,2},{4,3},{5,4},{6,5},{7,6},{8,15},{9,8},{10,9... | collective-permute-start | bytes 9437192 | tf_op jit(solution)/shard_map/ppermute | solution.py:24
  856.1 138.5 %copy-start.17 = (bf16[256,6144]{1,0:T(8,128)(2,1)}, bf16[256,6144]{1,0:T(8,128)(2,1)S(1)}, u32[]{:S(2)}) copy-start(bf16[256,6144]{1,0:T(8,128)(2,1)S(1)} %collective-permute-done.1) | copy-start | bytes 9437188
  856.1 274.9 %collective-permute-start.2 = (bf16[256,6144]{1,0:T(8,128)(2,1)S(1)}, bf16[256,6144]{1,0:T(8,128)(2,1)}, u32[]{:S(2)}, u32[]{:S(2)}) collective-permute-start(bf16[256,6144]{1,0:T(8,128)(2,1)S(1)} %collective-permute-done.1), channel_id=1, source_target_pairs={{0,1},{1,2},{2,3},{3,4},{4,5},{5,6},{6,7},{7,0},{8,9},{9,10},{10,1... | collective-permute-start | bytes 9437192 | tf_op jit(solution)/shard_map/ppermute | solution.py:22
  992.3 402.2 %collective-permute-start.5 = (bf16[256,6144]{1,0:T(8,128)(2,1)}, bf16[256,6144]{1,0:T(8,128)(2,1)}, u32[]{:S(2)}, u32[]{:S(2)}) collective-permute-start(bf16[256,6144]{1,0:T(8,128)(2,1)} %collective-permute-done.4), channel_id=1, source_target_pairs={{0,7},{1,0},{2,1},{3,2},{4,3},{5,4},{6,5},{7,6},{8,15},{9,8},{10,9... | collective-permute-start | bytes 9437192 | tf_op jit(solution)/shard_map/ppermute | solution.py:24
  1130.9 265.4 %collective-permute-start.3 = (bf16[256,6144]{1,0:T(8,128)(2,1)}, bf16[256,6144]{1,0:T(8,128)(2,1)}, u32[]{:S(2)}, u32[]{:S(2)}) collective-permute-start(bf16[256,6144]{1,0:T(8,128)(2,1)} %collective-permute-done.2), channel_id=1, source_target_pairs={{0,1},{1,2},{2,3},{3,4},{4,5},{5,6},{6,7},{7,0},{8,9},{9,10},{10,1... | collective-permute-start | bytes 9437192 | tf_op jit(solution)/shard_map/ppermute | solution.py:22
  1394.5 88.7 %collective-permute-start.6 = (bf16[256,6144]{1,0:T(8,128)(2,1)}, bf16[256,6144]{1,0:T(8,128)(2,1)S(1)}, u32[]{:S(2)}, u32[]{:S(2)}) collective-permute-start(bf16[256,6144]{1,0:T(8,128)(2,1)} %collective-permute-done.5), channel_id=1, source_target_pairs={{0,7},{1,0},{2,1},{3,2},{4,3},{5,4},{6,5},{7,6},{8,15},{9,8},{10,9... | collective-permute-start | bytes 9437192 | tf_op jit(solution)/shard_map/ppermute | solution.py:24
  1514.0 18.1 copy-start.19
  1532.1 28.7 copy-start.8
  1544.9 8.1 copy-start.47
  1553.1 7.7 copy-start.49
  1566.6 90.2 %copy-start.22 = (bf16[256,2048]{1,0:T(8,128)(2,1)S(1)}, bf16[256,2048]{1,0:T(8,128)(2,1)}, u32[]{:S(2)}) copy-start(bf16[256,2048]{1,0:T(8,128)(2,1)} %param.12) | copy-start | bytes 3145732
  1663.1 985.5 %copy-start.24 = (f32[256,2048]{1,0:T(8,128)}, f32[256,2048]{1,0:T(8,128)S(1)}, u32[]{:S(2)}) copy-start(f32[256,2048]{1,0:T(8,128)S(1)} %get-tuple-element.54) | copy-start | bytes 6291460
  1663.3 485.1 %copy-start.12 = (bf16[256,2048]{1,0:T(8,128)(2,1)}, bf16[256,2048]{1,0:T(8,128)(2,1)S(1)}, u32[]{:S(2)}) copy-start(bf16[256,2048]{1,0:T(8,128)(2,1)S(1)} %multiply_convert_fusion.5) | copy-start | bytes 3145732
  2633.7 14.9 copy-start.29
  2651.0 8.5 copy-start.5
  2651.0 9.0 copy-start.48
  2651.0 9.0 copy-start.50
  2660.6 14.7 slice-start
  2660.6 14.7 slice-start.1
  2660.6 15.9 slice-start.2
  2660.7 17.1 slice-start.3
  2677.7 10.3 copy-start.20
  2688.0 7.8 copy-start.55
  2688.0 8.4 copy-start.57
  2695.8 90.8 %reduce-scatter.7.cloned.1.call-start = ((), (), s32[]{:S(2)}) async-start(), calls=%async_computation.12 | async-start | bytes 2621440 | tf_op jit(solution)/shard_map/reduce_scatter | solution.py:293
  2704.5 4.2 copy-start.9
  2708.6 656.1 %reduce-scatter.9.cloned.1.call-start = ((), (), s32[]{:S(2)}) async-start(), calls=%async_computation.13 | async-start | bytes 37748736 | tf_op jit(solution)/shard_map/reduce_scatter | solution.py:331
  2714.6 5.1 copy-start.34
  2714.6 5.1 copy-start.36
  2725.5 4.8 copy-start.6
  2725.5 4.8 copy-start.32
  2730.3 56.2 %copy-start.31 = (bf16[256,2048]{1,0:T(8,128)(2,1)}, bf16[256,2048]{1,0:T(8,128)(2,1)S(1)}, u32[]{:S(2)}) copy-start(bf16[256,2048]{1,0:T(8,128)(2,1)S(1)} %get-tuple-element.27) | copy-start | bytes 3145732
  2749.1 37.4 copy-start.23
  2749.2 37.4 copy-start.44
  2749.2 37.4 copy-start.46
  2752.2 46.9 copy-start.38
  2822.0 1724.1 %reduce-scatter.11.cloned.1.call-start = ((), (), s32[]{:S(2)}) async-start(), calls=%async_computation.14 | async-start | bytes 84934656 | tf_op jit(solution)/shard_map/reduce_scatter | solution.py:235
  2837.1 14.0 copy-start.30
  2916.0 1871.2 %all-reduce.4.cloned.1.call-start = ((), (), s32[]{:S(2)}) async-start(), calls=%async_computation.15 | async-start | bytes 27262976 | tf_op jit(solution)/shard_map/psum | solution.py:80
  4547.6 15.0 copy-start.53
  4562.6 14.9 copy-start.58
  4562.6 56.9 %copy-start.7 = (f32[256,2048]{1,0:T(8,128)S(1)}, f32[256,2048]{1,0:T(8,128)}, u32[]{:S(2)}) copy-start(f32[256,2048]{1,0:T(8,128)} %copy-done.5) | copy-start | bytes 6291460
  4787.3 8.7 copy-start.1
  (23 other events, 53.9 us)
Sparse Core Ops, SparseCore 0:
  9.6 483.1 all-gather.9
  494.3 871.8 all-gather.19
  1368.4 65.2 all-gather.11
  1435.7 95.9 all-gather.13
  1533.6 123.1 all-gather.15
  1658.2 478.5 all-gather.17
  2138.4 481.6 all-gather.21
  2695.9 44.9 reduce-scatter.4
  2743.3 43.1 reduce-scatter.6
  2822.1 542.6 reduce-scatter.8
  3368.6 1177.3 reduce-scatter.10
  4548.7 238.5 all-reduce.3
